TPU v7x, 1024 devices: a whole 8x8x8 slice. The times are simulated.
1024 devices in a mesh: blk: 8 (over x), wide: 128 (over y, z, core).
Axes of the slice: x: 8, y: 8, z: 8, core: 2. Of those that a mesh axis runs over, the one named last changes fastest.
Arguments:
- upstream: bfloat16 [49152, 7168], P('wide'), may hold values from -8 to 8
- gate_pre: bfloat16 [49152, 1024], P('wide', 'blk'), may hold values from -6 to 6
- up_pre: bfloat16 [49152, 1024], P('wide', 'blk'), may hold values from -8 to 8
- down_weight: bfloat16 [7168, 2, 1024], P(None, None, 'blk'), may hold values from -0.1875 to 0.1875
- block_expert: int32 [384], P('wide'), may hold values from 0 to 1
- row_token: int32 [49152], P('wide'), may hold values from 0 to 383, as said below
- gate_prob: float32 [49152], P('wide'), may hold values from 0.05 to 0.8
Outputs:
- down_grad: float32 [7168, 2, 1024], P('wide', None, 'blk')
- grad_rms: float32 [2], replicated
- prob_grad: float32 [49152], P('wide')
- gate_grad: bfloat16 [49152, 1024], P('wide', 'blk')
- up_grad: bfloat16 [49152, 1024], P('wide', 'blk')
Inputs may be any that keep to these rules, and one draw needn't show every extreme that they name: Within each index of wide, row_token is a permutation of the 384 tokens held there: every token has exactly one routed row in the window.
All inputs are finite; a program needn't handle non-finite values.
Results may differ from a plain program's by a relative error of at most 0.0029.
Values sent between devices are 32-bit elements; how exact they have to be, the bound alone decides.
A program may use at most 64 MiB of HBM per device.

v0:
```python
import jax
import jax.numpy as jnp
from jax import lax
from jax.sharding import PartitionSpec as P

D = 7168
FFW = 1024
EXPERTS = 2
BLOCK = 128


def body(upstream, gate_pre, up_pre, down_weight, block_expert, row_token, gate_prob):
    routed = upstream[row_token]
    row_count = routed.shape[0]
    block_count = row_count // BLOCK
    width = routed.shape[1]
    hidden_share = gate_pre.shape[1]
    gate_value = gate_pre.astype(jnp.float32)
    up_value = up_pre.astype(jnp.float32)
    sigmoid_gate = jax.nn.sigmoid(gate_value)
    active = gate_value * sigmoid_gate
    hidden = active * up_value
    weighted = (hidden * gate_prob[:, None]).astype(jnp.bfloat16)
    routed_blocks = routed.reshape(block_count, BLOCK, width)
    weighted_blocks = weighted.reshape(block_count, BLOCK, hidden_share)

    def project(block_item):
        rows_block, expert_id = block_item
        weights = lax.dynamic_index_in_dim(down_weight, expert_id, 1, keepdims=False)
        return jnp.dot(rows_block, weights, preferred_element_type=jnp.float32)

    projected = lax.map(project, (routed_blocks, block_expert)).reshape(row_count, hidden_share)
    scaled = gate_prob[:, None] * projected
    up_grad = (scaled * active).astype(jnp.bfloat16)
    gate_grad = (
        scaled * up_value * sigmoid_gate * (1.0 + gate_value * (1.0 - sigmoid_gate))
    ).astype(jnp.bfloat16)
    partial_value = jnp.sum(hidden * projected, axis=1)
    prob_grad = lax.psum(partial_value, "blk")
    row_share = width // lax.axis_size("wide")

    def select_columns(amount):
        return routed.reshape(block_count, BLOCK, amount)

    def block_product(columns, block_index):
        column_block = lax.dynamic_index_in_dim(columns, block_index, 0, keepdims=False)
        weighted_block = lax.dynamic_index_in_dim(weighted_blocks, block_index, 0, keepdims=False)
        return jnp.dot(column_block.T, weighted_block, preferred_element_type=jnp.float32)

    pieces = []
    for expert in range(EXPERTS):

        def one_expert(first, amount, expert=expert):
            columns = select_columns(amount)

            def add_block(block_index, running):
                expert_id = lax.dynamic_index_in_dim(block_expert, block_index, 0, keepdims=False)

                def with_block(running_sum):
                    return running_sum + block_product(columns, block_index)

                def without_block(running_sum):
                    return running_sum

                return lax.cond(expert_id == expert, with_block, without_block, running)

            start_value = jnp.zeros((amount, hidden_share), jnp.float32)
            return lax.fori_loop(0, block_count, add_block, start_value)

        pieces.append(
            lax.psum_scatter(
                one_expert(jnp.int32(0), lax.axis_size("wide") * row_share),
                "wide",
                scatter_dimension=0,
                tiled=True,
            )
        )
    down_grad = jnp.stack(pieces, axis=1)
    squares = jnp.sum(down_grad * down_grad, axis=(0, 2))
    total_sum = lax.psum(squares, ("blk", "wide"))
    grad_rms = jnp.sqrt(total_sum / float(D * FFW))
    return (down_grad, grad_rms, prob_grad, gate_grad, up_grad)


def solution(mesh):
    in_specs = (
        P("wide", None),
        P("wide", "blk"),
        P("wide", "blk"),
        P(None, None, "blk"),
        P("wide"),
        P("wide"),
        P("wide"),
    )
    out_specs = (P("wide", None, "blk"), P(), P("wide"), P("wide", "blk"), P("wide", "blk"))
    return jax.shard_map(body, mesh=mesh, in_specs=in_specs, out_specs=out_specs, check_vma=False)
```

profile of v0, /device:TPU:1, one launch (start us, length us, event | category | flops | bytes accessed | tf_op | source)
XLA Modules:
  0.0 596.7 jit_solution(590728206749698457)
XLA Ops:
  7.2 0.7 compare_select_fusion
  7.9 4.4 copy.13
  12.3 16.5 %gather_fusion = bf16[384,7168]{1,0:T(8,128)(2,1)} fusion(bf16[384,7168]{1,0:T(8,128)(2,1)} %param.17, s32[1024]{0:T(1024)S(1)} %pad_clamp_fusion), kind=kCustom, calls=%fused_computation | custom fusion | bytes 11011584 | tf_op jit(solution)/shard_map/gather | solution.py:13
  28.8 15.7 %while.44 = (s32[]{:T(128)}, f32[3,128,128]{2,1,0:T(8,128)S(1)}, bf16[3,128,7168]{2,1,0:T(8,128)(2,1)}, s32[3]{0:T(128)S(1)}, bf16[7168,2,128]{2,0,1:T(8,128)(2,1)}, /*index=5*/s32[]{:T(128)}, s32[]{:T(128)}, s32[]{:T(128)}) while((s32[]{:T(128)}, f32[3,128,128]{2,1,0:T(8,128)S(1)}, bf16[3,128,7168]{2,1,0:T(8,128)(2,1)}, s32[3]{0:T(128)S(1)}, ...), condition=%wide.region_13.14_spmd, body=%wide.region_12.13_spmd.sunk | while | flops 234881024 | bytes 3736711 | solution.py:32
  31.3 2.7 fusion.39
  36.6 2.7 fusion.39
  41.8 2.7 fusion.39
  44.5 0.9 fusion.28
  45.4 2.1 broadcast.11.clone.1
  47.5 19.1 %while.42 = (s32[]{:T(128)}, f32[7168,128]{1,0:T(8,128)}, s32[3]{0:T(128)S(1)}, bf16[3,128,7168]{2,1,0:T(8,128)(2,1)}, bf16[3,128,128]{2,1,0:T(8,128)(2,1)S(1)}, /*index=5*/s32[]{:T(128)}, s32[1]{0:T(128)}) while((s32[]{:T(128)}, f32[7168,128]{1,0:T(8,128)}, s32[3]{0:T(128)S(1)}, bf16[3,128,7168]{2,1,0:T(8,128)(2,1)}, ...), condition=%wide.region_3.4_spmd, body=%wide.region_0.3_spmd.sunk | while | flops 235798528 | bytes 9209009 | solution.py:68
  48.7 5.1 conditional.4
  48.7 5.1 convolution_add_fusion
  55.0 5.1 conditional.4
  55.1 5.1 convolution_add_fusion
  61.4 5.1 conditional.4
  61.4 5.1 convolution_add_fusion
  66.6 2.1 broadcast.11.clone
  68.7 3.8 while.43
  72.5 14.7 %psum.15 = f32[384]{0:T(512)} all-reduce(f32[384]{0:T(512)S(1)} %get-tuple-element.309), channel_id=1, replica_groups=mesh['blk'=8,'wide'=128] {'blk'}, use_global_device_ids=true, to_apply=%region_15.16 | all-reduce | flops 384 | bytes 3072 | tf_op jit(solution)/shard_map/psum | solution.py:39
  87.2 184.2 %reduce-scatter.7.cloned.1.call-done = f32[56,128]{1,0:T(8,128)} async-done(((f32[7168,128]{1,0:T(8,128)}), f32[56,128]{1,0:T(8,128)}) %reduce-scatter.7.cloned.1.call-update) | async-done | bytes 28688
  271.4 200.6 %reduce-scatter.9.cloned.1.call-done = f32[56,128]{1,0:T(8,128)} async-done(((f32[7168,128]{1,0:T(8,128)}), f32[56,128]{1,0:T(8,128)}) %reduce-scatter.9.cloned.1.call-update) | async-done | bytes 28688
  471.9 0.9 multiply_reduce_fusion
  472.8 0.7 copy.14
  473.5 115.9 %psum.14 = f32[2]{0:T(128)S(1)} all-reduce(f32[2]{0:T(128)S(1)} %get-tuple-element.312), channel_id=1, replica_groups=mesh['blk'=8,'wide'=128] {'blk','wide'}, use_global_device_ids=true, to_apply=%region_11.12 | all-reduce | flops 2 | bytes 16 | tf_op jit(solution)/shard_map/psum | solution.py:80
  (27 shorter events, 6.0 us)
Async XLA Ops:
  7.2 264.2 %reduce-scatter.7.cloned.1.call-start = ((), (), s32[]{:S(2)}) async-start(), calls=%async_computation.2 | async-start | bytes 3698688
  12.3 16.5 %copy-start.3 = (s32[3]{0:T(128)S(1)}, s32[3]{0:T(128)}, u32[]{:S(2)}) copy-start(s32[3]{0:T(128)} %param.21) | copy-start | bytes 40
  28.8 15.7 %copy-start = (bf16[384,128]{1,0:T(8,128)(2,1)S(1)}, bf16[384,128]{1,0:T(8,128)(2,1)}, u32[]{:S(2)}) copy-start(bf16[384,128]{1,0:T(8,128)(2,1)} %param.19) | copy-start | bytes 294916
  28.8 15.7 %copy-start.1 = (bf16[384,128]{1,0:T(8,128)(2,1)S(1)}, bf16[384,128]{1,0:T(8,128)(2,1)}, u32[]{:S(2)}) copy-start(bf16[384,128]{1,0:T(8,128)(2,1)} %param.18) | copy-start | bytes 294916
  28.8 15.7 %copy-start.2 = (f32[384]{0:T(512)S(1)}, f32[384]{0:T(512)}, u32[]{:S(2)}) copy-start(f32[384]{0:T(512)} %param.23) | copy-start | bytes 4612
  66.5 405.4 %reduce-scatter.9.cloned.1.call-start = ((), (), s32[]{:S(2)}) async-start(), calls=%async_computation.3 | async-start | bytes 3698688
Sparse Core Ops, SparseCore 0:
  66.7 204.6 reduce-scatter.6
  277.0 194.8 reduce-scatter.8
where the time goes:
time: 597 us
  waiting for transfers between devices  385 us (64%)
  blocking collectives  131 us (22%)
  local copies, waits for them, and re-layouts  31 us (5%)
  matrix products  23.3 us (4%)
  between operations  14.1 us (2%)
  loops' own time  9.97 us (2%)
    unnamed x4, waiting for transfers between devices  385 us
    psum x1, blocking collectives, body(): total_sum = lax.psum(squares, ('blk', 'wide'))  116 us
    gather x1, local copies, waits for them, and re-layouts, body(): routed = upstream[row_token]  16.5 us
    dot_general x3, matrix products, block_product(): jnp.dot(column_block.T, weighted_block, preferred_element_type=jnp.float32)  15.3 us
    psum x1, blocking collectives, body(): prob_grad = lax.psum(partial_value, 'blk')  14.7 us
  transfers between devices with their start and end apart: 2, of which 2 were waited for; matrix products, arithmetic and copies ran while one was open for 1% of the time, Pallas kernels for 0%

commit v1 on v0

v1 whole, which is shorter than its diff:
```python
import functools

import jax
import jax.numpy as jnp
from jax import lax
from jax.experimental import pallas as pl
from jax.experimental.pallas import tpu as pltpu
from jax.sharding import PartitionSpec as P

D = 7168
FFW = 1024
BLOCK = 128
ROWS = 384
NBLK = 3
F = 128
SIDE = 8
PIECE = 56
COLS = 896
F32 = jnp.float32
BF16 = jnp.bfloat16
MESH = pl.DeviceIdType.MESH


def ring_offset(j):
    far = 4 - (j + 1) // 2
    odd = j % 2
    return (odd * far + (1 - odd) * (8 - far)) % 8


def across(row):
    return jnp.transpose(jnp.broadcast_to(row, (F, F)))


def kernel(
    u_hbm, w_hbm, gate_ref, up_ref, prob_ref, tok_ref, expert_ref,
    down_ref, rms_ref, pgrad_ref, ggrad_ref, ugrad_ref,
    ub, wv, g, r0, rc1, rc2, wf, pacc, wp, oh, pslot, qxc, qy, qz,
    usem, wsem, pair_send, r0_sem, ring_send, rc1_sem, rc2_sem,
    p_send, p_recv, xc_send, xc_recv, y_send, y_recv, z_send, z_recv,
):
    x = lax.axis_index("blk")
    wide = lax.axis_index("wide")
    c = wide % 2
    chip = wide // 2
    y = chip // SIDE
    z = chip % SIDE
    p = (1 - c) * y + c * z
    q = (1 - c) * z + c * y
    a = 8 - 7 * c
    b = 1 + 7 * c

    def block_copy(i):
        yi = (y + ring_offset(i)) % SIDE
        cols = pl.ds(pl.multiple_of(yi * COLS, 128), COLS)
        return pltpu.make_async_copy(u_hbm.at[:, cols], ub.at[i], usem.at[i])

    @pl.loop(0, SIDE)
    def _(i):
        block_copy(i).start()

    w_copy = pltpu.make_async_copy(w_hbm, wv, wsem)
    w_copy.start()

    barrier = pltpu.get_barrier_semaphore()

    def greet(xi, wi):
        pl.semaphore_signal(barrier, inc=1, device_id=(xi, wi), device_id_type=MESH)

    @pl.loop(1, SIDE)
    def _(o):
        greet((x + o) % SIDE, wide)
        greet((x + o) % SIDE, chip * 2 + 1 - c)
        greet(x, (((y + o) % SIDE) * SIDE + z) * 2 + c)
        greet(x, (y * SIDE + (z + o) % SIDE) * 2 + c)

    greet(x, chip * 2 + 1 - c)

    total = jnp.zeros((ROWS, 2 * F), F32)
    token_iota = lax.broadcasted_iota(jnp.int32, (ROWS, F), 0)
    for k in range(NBLK):
        rows = pl.ds(k * BLOCK, BLOCK)
        gate = gate_ref[rows, :].astype(F32)
        up = up_ref[rows, :].astype(F32)
        hidden = gate * jax.nn.sigmoid(gate) * up
        weighted = (hidden * across(prob_ref[pl.ds(k, 1), :])).astype(BF16).astype(F32)
        expert = jnp.full((F, F), expert_ref[k], jnp.int32)
        both = jnp.concatenate(
            [jnp.where(expert == e, weighted, 0.0) for e in range(2)], axis=1
        ).astype(BF16)
        hot = jnp.where(token_iota == tok_ref[pl.ds(k, 1), :], 1.0, 0.0).astype(BF16)
        oh[k] = hot
        total = total + jnp.dot(hot, both, preferred_element_type=F32)
    wp[...] = total.astype(BF16)

    pl.semaphore_wait(barrier, 4 * (SIDE - 1) + 1)

    def pair_copy(idx):
        return pltpu.make_async_remote_copy(
            src_ref=g.at[idx, 1 - c],
            dst_ref=r0.at[idx],
            send_sem=pair_send,
            recv_sem=r0_sem.at[idx],
            device_id=(x, chip * 2 + 1 - c),
            device_id_type=MESH,
        )

    @pl.loop(0, SIDE)
    def _(i):
        block_copy(i).wait()
        yi = (y + ring_offset(i)) % SIDE
        value = lax.dot_general(
            ub[i], wp[...], (((0,), (0,)), ((), ())), preferred_element_type=F32
        )
        g[pl.ds(yi * SIDE, SIDE)] = value.reshape(SIDE, 2, PIECE, 2 * F)

        @pl.loop(0, SIDE)
        def _(zi):
            pair_copy(yi * SIDE + zi).start()

    w_copy.wait()
    pacc[...] = jnp.zeros_like(pacc)

    def slot(d, k, j):
        return (d * 4 + k - 1) * SIDE + j

    def first_copy(d, k, j, idx):
        step = 1 if d == 0 else SIDE - 1
        to = (a * ((p + step) % SIDE) + b * q) * 2 + c
        s = slot(d, k, j)
        return pltpu.make_async_remote_copy(
            src_ref=r0.at[idx],
            dst_ref=rc1.at[s],
            send_sem=ring_send,
            recv_sem=rc1_sem.at[s],
            device_id=(x, to),
            device_id_type=MESH,
        )

    def first_send(d, k, j, more):
        step = 1 if d == 0 else SIDE - 1
        idx = a * ((p + step * k) % SIDE) + b * ((q + ring_offset(j)) % SIDE)
        pair_copy(idx).wait_recv()
        value = r0[idx] + g[idx, c]
        if more:
            first_copy(d, k + 1, j, idx).wait_recv()
            value = value + rc1[slot(d, k + 1, j)]
        r0[idx] = value
        first_copy(d, k, j, idx).start()

    def project(i):
        yi = (y + ring_offset(i)) % SIDE
        wf[...] = wv[pl.ds(pl.multiple_of(yi * 2 * COLS, 16), 2 * COLS), :].astype(F32)
        weight = jnp.concatenate(
            [wf[pl.ds(e, COLS, stride=2), :].astype(BF16) for e in range(2)], axis=1
        )
        pacc[...] += jnp.dot(ub[i], weight, preferred_element_type=F32)

    @pl.loop(0, 4)
    def _(j):
        first_send(0, 4, j + 4, False)
        first_send(1, 4, j, False)

    @pl.loop(0, 4)
    def _(j):
        first_send(0, 3, j, False)
        first_send(1, 3, j + 4, False)

    @pl.loop(0, 4)
    def _(j):
        first_send(0, 3, j + 4, True)
        first_send(1, 3, j, True)

    @pl.loop(0, 4)
    def _(j):
        for h in range(2):
            first_send(0, 2, 2 * j + h, True)
            first_send(1, 2, (2 * j + h + 4) % SIDE, True)
        project(j)

    @pl.loop(0, 4)
    def _(j):
        for h in range(2):
            first_send(0, 1, 2 * j + h, True)
            first_send(1, 1, 2 * j + h, True)
        project(j + 4)

    high = pacc[...].astype(BF16)
    rest = pacc[...] - high.astype(F32)
    middle = rest.astype(BF16)
    low = (rest - middle.astype(F32)).astype(BF16)
    pslot[x] = jnp.zeros((8, F), F32)
    for k in range(NBLK):
        rows = pl.ds(k * BLOCK, BLOCK)
        hot = oh[k]
        moved = sum(
            lax.dot_general(hot, term, (((0,), (0,)), ((), ())), preferred_element_type=F32)
            for term in (low, middle, high)
        )
        expert = jnp.full((F, F), expert_ref[k], jnp.int32)
        projected = jnp.where(expert == 0, moved[:, :F], moved[:, F:])
        gate = gate_ref[rows, :].astype(F32)
        up = up_ref[rows, :].astype(F32)
        sig = jax.nn.sigmoid(gate)
        active = gate * sig
        scaled = across(prob_ref[pl.ds(k, 1), :]) * projected
        ugrad_ref[rows, :] = (scaled * active).astype(BF16)
        ggrad_ref[rows, :] = (scaled * up * sig * (1.0 + gate * (1.0 - sig))).astype(BF16)
        part = jnp.transpose(active * up * projected)
        pslot[x, pl.ds(k, 1), :] = jnp.sum(part, axis=0, keepdims=True)

    def p_copy(s, to):
        return pltpu.make_async_remote_copy(
            src_ref=pslot.at[s],
            dst_ref=pslot.at[s],
            send_sem=p_send.at[to],
            recv_sem=p_recv.at[s],
            device_id=(to, wide),
            device_id_type=MESH,
        )

    @pl.loop(1, SIDE)
    def _(o):
        p_copy(x, (x + o) % SIDE).start()

    def second_slot(d, k):
        return d * 4 + k - 1

    def second_copy(d, k, idx):
        step = 1 if d == 0 else SIDE - 1
        to = (a * p + b * ((q + step) % SIDE)) * 2 + c
        s = second_slot(d, k)
        return pltpu.make_async_remote_copy(
            src_ref=r0.at[idx],
            dst_ref=rc2.at[s],
            send_sem=ring_send,
            recv_sem=rc2_sem.at[s],
            device_id=(x, to),
            device_id_type=MESH,
        )

    def own(j):
        idx = a * p + b * ((q + ring_offset(j)) % SIDE)
        pair_copy(idx).wait_recv()
        first_copy(0, 1, j, idx).wait_recv()
        first_copy(1, 1, j, idx).wait_recv()
        return idx, r0[idx] + g[idx, c] + rc1[slot(0, 1, j)] + rc1[slot(1, 1, j)]

    for j, d, k, more in (
        (0, 0, 4, False), (2, 1, 3, False), (1, 0, 3, True), (4, 1, 2, True),
        (3, 0, 2, True), (6, 1, 1, True), (5, 0, 1, True),
    ):
        idx, value = own(j)
        if more:
            second_copy(d, k + 1, idx).wait_recv()
            value = value + rc2[second_slot(d, k + 1)]
        r0[idx] = value
        second_copy(d, k, idx).start()
    idx, value = own(7)
    for d in range(2):
        second_copy(d, 1, idx).wait_recv()
        value = value + rc2[second_slot(d, 1)]
    down_ref[0] = value[:, :F]
    down_ref[1] = value[:, F:]
    square = jnp.sum((value * value).reshape(PIECE // 8, 8, 2 * F), axis=0)

    def gather(value, buf, mine, count, send, recv, where):
        buf[mine] = value

        def copy(s, to):
            return pltpu.make_async_remote_copy(
                src_ref=buf.at[s],
                dst_ref=buf.at[s],
                send_sem=send.at[to],
                recv_sem=recv.at[s],
                device_id=where(to),
                device_id_type=MESH,
            )

        @pl.loop(1, count)
        def _(o):
            copy(mine, (mine + o) % count).start()

        @pl.loop(1, count)
        def _(o):
            other = (mine + o) % count
            copy(other, other).wait_recv()

        result = jnp.sum(buf[...], axis=0)

        @pl.loop(1, count)
        def _(o):
            copy(mine, (mine + o) % count).wait_send()

        return result

    square = gather(
        square, qxc, x * 2 + c, 2 * SIDE, xc_send, xc_recv,
        lambda to: (to // 2, chip * 2 + to % 2),
    )
    square = gather(
        square, qy, y, SIDE, y_send, y_recv, lambda to: (x, (to * SIDE + z) * 2 + c)
    )
    square = gather(
        square, qz, z, SIDE, z_send, z_recv, lambda to: (x, (y * SIDE + to) * 2 + c)
    )
    lane = lax.broadcasted_iota(jnp.int32, (8, F), 1)
    rms = [jnp.sqrt(jnp.sum(square[:, e * F:(e + 1) * F]) / float(D * FFW)) for e in range(2)]
    rms_ref[...] = jnp.where(lane == 0, rms[0], rms[1])

    @pl.loop(1, SIDE)
    def _(o):
        other = (x + o) % SIDE
        p_copy(other, other).wait_recv()

    pgrad_ref[...] = jnp.sum(pslot[...], axis=0)

    @pl.loop(1, SIDE)
    def _(o):
        p_copy(x, (x + o) % SIDE).wait_send()

    pltpu.make_async_copy(r0, r0, pair_send).wait()
    pltpu.make_async_copy(r0.at[pl.ds(0, 63)], r0.at[pl.ds(0, 63)], ring_send).wait()


def body(upstream, gate_pre, up_pre, down_weight, block_expert, row_token, gate_prob):
    vmem = pl.BlockSpec(memory_space=pltpu.VMEM)
    any_space = pl.BlockSpec(memory_space=pl.ANY)
    dma = pltpu.SemaphoreType.DMA
    down, rms, pgrad, ggrad, ugrad = pl.pallas_call(
        kernel,
        name="experts_backward",
        out_shape=(
            jax.ShapeDtypeStruct((2, PIECE, F), F32),
            jax.ShapeDtypeStruct((8, F), F32),
            jax.ShapeDtypeStruct((8, F), F32),
            jax.ShapeDtypeStruct((ROWS, F), BF16),
            jax.ShapeDtypeStruct((ROWS, F), BF16),
        ),
        in_specs=[
            any_space, any_space, vmem, vmem, vmem, vmem,
            pl.BlockSpec(memory_space=pltpu.SMEM),
        ],
        out_specs=(vmem,) * 5,
        scratch_shapes=[
            pltpu.VMEM((SIDE, ROWS, COLS), BF16),
            pltpu.VMEM((2 * D, F), BF16),
            pltpu.VMEM((64, 2, PIECE, 2 * F), F32),
            pltpu.VMEM((64, PIECE, 2 * F), F32),
            pltpu.VMEM((64, PIECE, 2 * F), F32),
            pltpu.VMEM((8, PIECE, 2 * F), F32),
            pltpu.VMEM((2 * COLS, F), F32),
            pltpu.VMEM((ROWS, 2 * F), F32),
            pltpu.VMEM((ROWS, 2 * F), BF16),
            pltpu.VMEM((NBLK, ROWS, F), BF16),
            pltpu.VMEM((SIDE, 8, F), F32),
            pltpu.VMEM((2 * SIDE, 8, 2 * F), F32),
            pltpu.VMEM((SIDE, 8, 2 * F), F32),
            pltpu.VMEM((SIDE, 8, 2 * F), F32),
            dma((SIDE,)), dma, dma, dma((64,)), dma, dma((64,)), dma((8,)),
            dma((SIDE,)), dma((SIDE,)), dma((2 * SIDE,)), dma((2 * SIDE,)),
            dma((SIDE,)), dma((SIDE,)), dma((SIDE,)), dma((SIDE,)),
        ],
        compiler_params=pltpu.CompilerParams(
            collective_id=0, has_side_effects=True, vmem_limit_bytes=60 * 1024 * 1024
        ),
    )(
        upstream,
        down_weight.reshape(2 * D, F),
        gate_pre,
        up_pre,
        gate_prob.reshape(NBLK, BLOCK),
        row_token.reshape(NBLK, BLOCK),
        block_expert,
    )
    return (
        jnp.transpose(down, (1, 0, 2)),
        rms[0, :2],
        pgrad[:NBLK].reshape(ROWS),
        ggrad,
        ugrad,
    )


def solution(mesh):
    in_specs = (
        P("wide", None),
        P("wide", "blk"),
        P("wide", "blk"),
        P(None, None, "blk"),
        P("wide"),
        P("wide"),
        P("wide"),
    )
    out_specs = (P("wide", None, "blk"), P(), P("wide"), P("wide", "blk"), P("wide", "blk"))
    return jax.shard_map(body, mesh=mesh, in_specs=in_specs, out_specs=out_specs, check_vma=False)
```

time: 597 us -> 85 us (0.14)
  waiting for transfers between devices: 385 us -> 0 us
  blocking collectives: 131 us -> 0 us
  Pallas kernels: 0 us -> 77 us
  local copies, waits for them, and re-layouts: 31 us -> 7 us
  matrix products: 23.3 us -> 0 us
  between operations: 14.1 us -> 0.64 us
  loops' own time: 9.97 us -> 0 us
    unnamed x4 -> x0, waiting for transfers between devices: 385 us -> none
    psum x2 -> x0, blocking collectives: 131 us -> none  [the longest x1 116 us: body(): total_sum = lax.psum(squares, ('blk', 'wide'))]
    pallas_call x0 -> x1, Pallas kernels: none -> 77 us  [body(): pl.pallas_call(kernel, name='experts_backward', out_shape=(jax.ShapeDtype...]
    dot_general x6 -> x0, matrix products: 23.3 us -> none  [the longest x3 15.3 us: block_product(): jnp.dot(column_block.T, weighted_block, preferred_element_type=jnp.float32)]
    gather x1 -> x0, local copies, waits for them, and re-layouts: 16.5 us -> none  [body(): routed = upstream[row_token]]
    another operation x9 -> x0, loops' own time: 9.97 us -> none  [the longest x1 5.89 us: body(): lax.map(project, (routed_blocks, block_expert))]
  transfers between devices with their start and end apart: 2 -> 0, of which waited for: 2 -> 0; matrix products, arithmetic and copies ran while one was open for 1% -> 0% of each run, Pallas kernels for 0% -> 0%
where the time goes in v1:
time: 85 us; the launch traced here: 84.7 us
  Pallas kernels  77 us (91%)
  local copies, waits for them, and re-layouts  7 us (8%)
    pallas_call x1, Pallas kernels, body(): pl.pallas_call(kernel, name='experts_backward', out_shape=(jax.ShapeDtype...  77 us
    unnamed x3, local copies, waits for them, and re-layouts  4.55 us

profile of v1, /device:TPU:1, one launch (start us, length us, event | category | flops | bytes accessed | tf_op | source)
XLA Modules:
  0.0 84.7 jit_solution(12542348430539096)
XLA Ops:
  0.6 77.0 %experts_backward.1 = (f32[2,56,128]{2,1,0:T(8,128)}, f32[8,128]{1,0:T(8,128)}, f32[8,128]{1,0:T(8,128)}, bf16[384,128]{1,0:T(8,128)(2,1)}, bf16[384,128]{1,0:T(8,128)(2,1)}) custom-call(bf16[384,7168]{1,0:T(8,128)(2,1)} %u_hbm.1, bf16[14336,128]{1,0:T(8,128)(2,1)} %bitcast.8, bf16[384,128]{1,0:T(8,128)(2,1)} %gate_ref.1, bf16[384,128]{1,0:T(8,128)(2,1)} %up_ref.1, ...), custom_call_target="tpu_custom_call" | custom-call | tf_op jit(solution)/shard_map/experts_backward/pallas_call | solution.py:329
  77.6 1.5 %copy.12 = f32[56,2,128]{2,1,0:T(2,128)} copy(f32[56,2,128]{2,0,1:T(8,128)} %bitcast.9) | data formatting | bytes 114688
  79.1 1.2 %slice_bitcast_fusion.1 = f32[2]{0:T(128)} fusion(f32[8,128]{1,0:T(8,128)} %get-tuple-element.11), kind=kLoop, calls=%fused_computation.1 | loop fusion | bytes 16 | tf_op jit(solution)/shard_map/squeeze | solution.py:377
  80.3 1.3 %slice_bitcast_fusion = f32[384]{0:T(512)} fusion(f32[8,128]{1,0:T(8,128)} %get-tuple-element.12), kind=kLoop, calls=%fused_computation | loop fusion | bytes 3072 | tf_op jit(solution)/shard_map/reshape | solution.py:378
  81.6 1.5 %copy.15 = bf16[384,128]{1,0:T(8,128)(2,1)} copy(bf16[384,128]{1,0:T(8,128)(2,1)} %get-tuple-element.28) | data formatting | bytes 196608
  83.1 1.5 %copy.16 = bf16[384,128]{1,0:T(8,128)(2,1)} copy(bf16[384,128]{1,0:T(8,128)(2,1)} %get-tuple-element.29) | data formatting | bytes 196608

commit v2 on v1

--- a/solution.py
+++ b/solution.py
@@ -18,6 +18,7 @@
 COLS = 896
 F32 = jnp.float32
 BF16 = jnp.bfloat16
+VMEM_LIMIT = 60
 MESH = pl.DeviceIdType.MESH
 
 
@@ -32,10 +33,11 @@
 
 
 def kernel(
-    u_hbm, w_hbm, gate_ref, up_ref, prob_ref, tok_ref, expert_ref,
+    u_hbm, w_hbm, gate_hbm, up_hbm, prob_hbm, tok_hbm, expert_hbm,
     down_ref, rms_ref, pgrad_ref, ggrad_ref, ugrad_ref,
+    gate_ref, up_ref, prob_ref, tok_ref, expert_ref,
     ub, wv, g, r0, rc1, rc2, wf, pacc, wp, oh, pslot, qxc, qy, qz,
-    usem, wsem, pair_send, r0_sem, ring_send, rc1_sem, rc2_sem,
+    insem, usem, wsem, pair_send, r0_sem, ring_send, rc1_sem, rc2_sem,
     p_send, p_recv, xc_send, xc_recv, y_send, y_recv, z_send, z_recv,
 ):
     x = lax.axis_index("blk")
@@ -49,6 +51,16 @@
     a = 8 - 7 * c
     b = 1 + 7 * c
 
+    small = [
+        pltpu.make_async_copy(src, dst, insem.at[n])
+        for n, (src, dst) in enumerate((
+            (tok_hbm, tok_ref), (prob_hbm, prob_ref), (expert_hbm, expert_ref),
+            (gate_hbm, gate_ref), (up_hbm, up_ref),
+        ))
+    ]
+    for copy in small:
+        copy.start()
+
     def block_copy(i):
         yi = (y + ring_offset(i)) % SIDE
         cols = pl.ds(pl.multiple_of(yi * COLS, 128), COLS)
@@ -74,6 +86,9 @@
         greet(x, (y * SIDE + (z + o) % SIDE) * 2 + c)
 
     greet(x, chip * 2 + 1 - c)
+
+    for copy in small:
+        copy.wait()
 
     total = jnp.zeros((ROWS, 2 * F), F32)
     token_iota = lax.broadcasted_iota(jnp.int32, (ROWS, F), 0)
@@ -92,18 +107,6 @@
         total = total + jnp.dot(hot, both, preferred_element_type=F32)
     wp[...] = total.astype(BF16)
 
-    pl.semaphore_wait(barrier, 4 * (SIDE - 1) + 1)
-
-    def pair_copy(idx):
-        return pltpu.make_async_remote_copy(
-            src_ref=g.at[idx, 1 - c],
-            dst_ref=r0.at[idx],
-            send_sem=pair_send,
-            recv_sem=r0_sem.at[idx],
-            device_id=(x, chip * 2 + 1 - c),
-            device_id_type=MESH,
-        )
-
     @pl.loop(0, SIDE)
     def _(i):
         block_copy(i).wait()
@@ -113,15 +116,38 @@
         )
         g[pl.ds(yi * SIDE, SIDE)] = value.reshape(SIDE, 2, PIECE, 2 * F)
 
+    pl.semaphore_wait(barrier, 4 * (SIDE - 1) + 1)
+
+    def pair_copy(r, j, sem):
+        far, near = (other_p + ring_offset(r)) % SIDE, (other_q + ring_offset(j)) % SIDE
+        idx = b * far + a * near
+        return pltpu.make_async_remote_copy(
+            src_ref=g.at[idx, 1 - c],
+            dst_ref=r0.at[idx],
+            send_sem=pair_send,
+            recv_sem=r0_sem.at[sem],
+            device_id=(x, chip * 2 + 1 - c),
+            device_id_type=MESH,
+        )
+
+    other_p, other_q = q, p
+
+    @pl.loop(0, SIDE)
+    def _(j):
+        pair_copy(0, j, j).start()
+
+    @pl.loop(1, SIDE)
+    def _(r):
         @pl.loop(0, SIDE)
-        def _(zi):
-            pair_copy(yi * SIDE + zi).start()
-
-    w_copy.wait()
-    pacc[...] = jnp.zeros_like(pacc)
+        def _(j):
+            pair_copy(r, j, SIDE - 1 + r).start()
+
+    def pair_wait(sem, pieces):
+        part = r0.at[pl.ds(0, pieces)]
+        pltpu.make_async_copy(part, part, r0_sem.at[sem]).wait()
 
     def slot(d, k, j):
-        return (d * 4 + k - 1) * SIDE + j
+        return 6 * SIDE + j if k == 4 else (d * 3 + k - 1) * SIDE + j
 
     def first_copy(d, k, j, idx):
         step = 1 if d == 0 else SIDE - 1
@@ -139,7 +165,8 @@
     def first_send(d, k, j, more):
         step = 1 if d == 0 else SIDE - 1
         idx = a * ((p + step * k) % SIDE) + b * ((q + ring_offset(j)) % SIDE)
-        pair_copy(idx).wait_recv()
+        if k == 4:
+            pair_wait(j, 1)
         value = r0[idx] + g[idx, c]
         if more:
             first_copy(d, k + 1, j, idx).wait_recv()
@@ -160,29 +187,48 @@
         first_send(0, 4, j + 4, False)
         first_send(1, 4, j, False)
 
+    pair_wait(SIDE, SIDE)
+    pair_wait(SIDE + 1, SIDE)
+
     @pl.loop(0, 4)
     def _(j):
         first_send(0, 3, j, False)
         first_send(1, 3, j + 4, False)
 
+    w_copy.wait()
+    pacc[...] = jnp.zeros_like(pacc)
+
     @pl.loop(0, 4)
     def _(j):
         first_send(0, 3, j + 4, True)
         first_send(1, 3, j, True)
+        project(j)
+
+    pair_wait(SIDE + 2, SIDE)
+    pair_wait(SIDE + 3, SIDE)
 
     @pl.loop(0, 4)
     def _(j):
         for h in range(2):
             first_send(0, 2, 2 * j + h, True)
             first_send(1, 2, (2 * j + h + 4) % SIDE, True)
-        project(j)
-
-    @pl.loop(0, 4)
-    def _(j):
-        for h in range(2):
-            first_send(0, 1, 2 * j + h, True)
-            first_send(1, 1, 2 * j + h, True)
         project(j + 4)
+
+    def exchange(buf, mine, count, send, recv, where):
+        @pl.loop(1, count)
+        def _(o):
+            pltpu.make_async_remote_copy(
+                src_ref=buf.at[mine],
+                dst_ref=buf.at[mine],
+                send_sem=send,
+                recv_sem=recv,
+                device_id=where((mine + o) % count),
+                device_id_type=MESH,
+            ).start()
+
+    def exchanged(buf, count, sem):
+        part = buf.at[pl.ds(0, count - 1)]
+        pltpu.make_async_copy(part, part, sem).wait()
 
     high = pacc[...].astype(BF16)
     rest = pacc[...] - high.astype(F32)
@@ -208,19 +254,17 @@
         part = jnp.transpose(active * up * projected)
         pslot[x, pl.ds(k, 1), :] = jnp.sum(part, axis=0, keepdims=True)
 
-    def p_copy(s, to):
-        return pltpu.make_async_remote_copy(
-            src_ref=pslot.at[s],
-            dst_ref=pslot.at[s],
-            send_sem=p_send.at[to],
-            recv_sem=p_recv.at[s],
-            device_id=(to, wide),
-            device_id_type=MESH,
-        )
-
-    @pl.loop(1, SIDE)
-    def _(o):
-        p_copy(x, (x + o) % SIDE).start()
+    exchange(pslot, x, SIDE, p_send, p_recv, lambda to: (to, wide))
+
+    pair_wait(SIDE + 4, SIDE)
+    pair_wait(SIDE + 5, SIDE)
+
+    @pl.loop(0, SIDE)
+    def _(j):
+        first_send(0, 1, j, True)
+        first_send(1, 1, j, True)
+
+    pair_wait(SIDE + 6, SIDE)
 
     def second_slot(d, k):
         return d * 4 + k - 1
@@ -240,7 +284,6 @@
 
     def own(j):
         idx = a * p + b * ((q + ring_offset(j)) % SIDE)
-        pair_copy(idx).wait_recv()
         first_copy(0, 1, j, idx).wait_recv()
         first_copy(1, 1, j, idx).wait_recv()
         return idx, r0[idx] + g[idx, c] + rc1[slot(0, 1, j)] + rc1[slot(1, 1, j)]
@@ -261,107 +304,83 @@
         value = value + rc2[second_slot(d, 1)]
     down_ref[0] = value[:, :F]
     down_ref[1] = value[:, F:]
-    square = jnp.sum((value * value).reshape(PIECE // 8, 8, 2 * F), axis=0)
-
-    def gather(value, buf, mine, count, send, recv, where):
-        buf[mine] = value
-
-        def copy(s, to):
-            return pltpu.make_async_remote_copy(
-                src_ref=buf.at[s],
-                dst_ref=buf.at[s],
-                send_sem=send.at[to],
-                recv_sem=recv.at[s],
-                device_id=where(to),
-                device_id_type=MESH,
-            )
-
-        @pl.loop(1, count)
-        def _(o):
-            copy(mine, (mine + o) % count).start()
-
-        @pl.loop(1, count)
-        def _(o):
-            other = (mine + o) % count
-            copy(other, other).wait_recv()
-
-        result = jnp.sum(buf[...], axis=0)
-
-        @pl.loop(1, count)
-        def _(o):
-            copy(mine, (mine + o) % count).wait_send()
-
-        return result
-
-    square = gather(
-        square, qxc, x * 2 + c, 2 * SIDE, xc_send, xc_recv,
-        lambda to: (to // 2, chip * 2 + to % 2),
+    column = jnp.sum(value * value, axis=0, keepdims=True)
+    square = jnp.concatenate([column[:, :F], column[:, F:]], axis=0)
+
+    stages = (
+        (qxc, x * 2 + c, 2 * SIDE, xc_send, xc_recv, lambda to: (to // 2, chip * 2 + to % 2)),
+        (qy, y, SIDE, y_send, y_recv, lambda to: (x, (to * SIDE + z) * 2 + c)),
+        (qz, z, SIDE, z_send, z_recv, lambda to: (x, (y * SIDE + to) * 2 + c)),
     )
-    square = gather(
-        square, qy, y, SIDE, y_send, y_recv, lambda to: (x, (to * SIDE + z) * 2 + c)
-    )
-    square = gather(
-        square, qz, z, SIDE, z_send, z_recv, lambda to: (x, (y * SIDE + to) * 2 + c)
-    )
-    lane = lax.broadcasted_iota(jnp.int32, (8, F), 1)
-    rms = [jnp.sqrt(jnp.sum(square[:, e * F:(e + 1) * F]) / float(D * FFW)) for e in range(2)]
-    rms_ref[...] = jnp.where(lane == 0, rms[0], rms[1])
-
-    @pl.loop(1, SIDE)
-    def _(o):
-        other = (x + o) % SIDE
-        p_copy(other, other).wait_recv()
-
+    for buf, mine, count, send, recv, where in stages:
+        buf[mine] = square
+        exchange(buf, mine, count, send, recv, where)
+        exchanged(buf, count, recv)
+        square = jnp.sum(buf[...], axis=0)
+    mean = jnp.sum(square, axis=1, keepdims=True) / float(D * FFW)
+    rms_ref[...] = jnp.broadcast_to(jnp.sqrt(mean), (2, F))
+
+    exchanged(pslot, SIDE, p_recv)
     pgrad_ref[...] = jnp.sum(pslot[...], axis=0)
 
-    @pl.loop(1, SIDE)
-    def _(o):
-        p_copy(x, (x + o) % SIDE).wait_send()
-
+    exchanged(pslot, SIDE, p_send)
+    for buf, _, count, send, _, _ in stages:
+        exchanged(buf, count, send)
     pltpu.make_async_copy(r0, r0, pair_send).wait()
     pltpu.make_async_copy(r0.at[pl.ds(0, 63)], r0.at[pl.ds(0, 63)], ring_send).wait()
 
 
+def place(down_ref, rms_ref, pgrad_ref, ggrad_ref, ugrad_ref, down, rms, pgrad, ggrad, ugrad):
+    for e in range(2):
+        down[:, e, :] = down_ref[e]
+    lane = lax.broadcasted_iota(jnp.int32, (1, F), 1)
+    rms[...] = jnp.where(lane == 0, rms_ref[0:1, :], rms_ref[1:2, :])[:, :2]
+    pgrad[...] = pgrad_ref[0:NBLK, :]
+    ggrad[...] = ggrad_ref[...]
+    ugrad[...] = ugrad_ref[...]
+
+
 def body(upstream, gate_pre, up_pre, down_weight, block_expert, row_token, gate_prob):
     vmem = pl.BlockSpec(memory_space=pltpu.VMEM)
-    any_space = pl.BlockSpec(memory_space=pl.ANY)
+    hbm = pl.BlockSpec(memory_space=pl.ANY)
     dma = pltpu.SemaphoreType.DMA
-    down, rms, pgrad, ggrad, ugrad = pl.pallas_call(
+    results = pl.pallas_call(
         kernel,
         name="experts_backward",
         out_shape=(
             jax.ShapeDtypeStruct((2, PIECE, F), F32),
-            jax.ShapeDtypeStruct((8, F), F32),
+            jax.ShapeDtypeStruct((2, F), F32),
             jax.ShapeDtypeStruct((8, F), F32),
             jax.ShapeDtypeStruct((ROWS, F), BF16),
             jax.ShapeDtypeStruct((ROWS, F), BF16),
         ),
-        in_specs=[
-            any_space, any_space, vmem, vmem, vmem, vmem,
-            pl.BlockSpec(memory_space=pltpu.SMEM),
-        ],
+        in_specs=[hbm] * 7,
         out_specs=(vmem,) * 5,
         scratch_shapes=[
+            pltpu.VMEM((ROWS, F), BF16),
+            pltpu.VMEM((ROWS, F), BF16),
+            pltpu.VMEM((NBLK, BLOCK), F32),
+            pltpu.VMEM((NBLK, BLOCK), jnp.int32),
+            pltpu.SMEM((NBLK,), jnp.int32),
             pltpu.VMEM((SIDE, ROWS, COLS), BF16),
             pltpu.VMEM((2 * D, F), BF16),
             pltpu.VMEM((64, 2, PIECE, 2 * F), F32),
             pltpu.VMEM((64, PIECE, 2 * F), F32),
-            pltpu.VMEM((64, PIECE, 2 * F), F32),
+            pltpu.VMEM((56, PIECE, 2 * F), F32),
             pltpu.VMEM((8, PIECE, 2 * F), F32),
             pltpu.VMEM((2 * COLS, F), F32),
             pltpu.VMEM((ROWS, 2 * F), F32),
             pltpu.VMEM((ROWS, 2 * F), BF16),
             pltpu.VMEM((NBLK, ROWS, F), BF16),
             pltpu.VMEM((SIDE, 8, F), F32),
-            pltpu.VMEM((2 * SIDE, 8, 2 * F), F32),
-            pltpu.VMEM((SIDE, 8, 2 * F), F32),
-            pltpu.VMEM((SIDE, 8, 2 * F), F32),
-            dma((SIDE,)), dma, dma, dma((64,)), dma, dma((64,)), dma((8,)),
-            dma((SIDE,)), dma((SIDE,)), dma((2 * SIDE,)), dma((2 * SIDE,)),
-            dma((SIDE,)), dma((SIDE,)), dma((SIDE,)), dma((SIDE,)),
+            pltpu.VMEM((2 * SIDE, 2, F), F32),
+            pltpu.VMEM((SIDE, 2, F), F32),
+            pltpu.VMEM((SIDE, 2, F), F32),
+            dma((5,)), dma((SIDE,)), dma, dma, dma((2 * SIDE - 1,)), dma, dma((56,)), dma((8,)),
+            dma, dma, dma, dma, dma, dma, dma, dma,
         ],
         compiler_params=pltpu.CompilerParams(
-            collective_id=0, has_side_effects=True, vmem_limit_bytes=60 * 1024 * 1024
+            collective_id=0, has_side_effects=True, vmem_limit_bytes=VMEM_LIMIT * 1024 * 1024
         ),
     )(
         upstream,
@@ -372,13 +391,20 @@
         row_token.reshape(NBLK, BLOCK),
         block_expert,
     )
-    return (
-        jnp.transpose(down, (1, 0, 2)),
-        rms[0, :2],
-        pgrad[:NBLK].reshape(ROWS),
-        ggrad,
-        ugrad,
-    )
+    down, rms, pgrad, ggrad, ugrad = pl.pallas_call(
+        place,
+        name="place_results",
+        out_shape=(
+            jax.ShapeDtypeStruct((PIECE, 2, F), F32),
+            jax.ShapeDtypeStruct((1, 2), F32),
+            jax.ShapeDtypeStruct((NBLK, BLOCK), F32),
+            jax.ShapeDtypeStruct((ROWS, F), BF16),
+            jax.ShapeDtypeStruct((ROWS, F), BF16),
+        ),
+        in_specs=[vmem] * 5,
+        out_specs=(vmem,) * 5,
+    )(*results)
+    return down, rms.reshape(2), pgrad.reshape(ROWS), ggrad, ugrad
 
 
 def solution(mesh):

time: 85 us -> 74.2 us (0.87)
  local copies, waits for them, and re-layouts: 7 us -> 0 us
  Pallas kernels: 77 us -> 73.4 us
    pallas_call x1, Pallas kernels: 77 us -> 71.7 us  [body(): pl.pallas_call(kernel, name='experts_backward', out_shape=(jax.ShapeDtype...]
    unnamed x3 -> x0, local copies, waits for them, and re-layouts: 4.55 us -> none
    pallas_call x0 -> x1, Pallas kernels: none -> 1.68 us  [body(): pl.pallas_call(place, name='place_results', out_shape=(jax.ShapeDtypeStru...]
    reshape x1 -> x0, local copies, waits for them, and re-layouts: 1.26 us -> none  [body(): pgrad[:NBLK].reshape(ROWS)]
    squeeze x1 -> x0, local copies, waits for them, and re-layouts: 1.19 us -> none  [body(): rms[0, :2]]
where the time goes in v2:
time: 74.2 us; the launch traced here: 74 us
  Pallas kernels  73.4 us (99%)
    pallas_call x1, Pallas kernels, body(): pl.pallas_call(kernel, name='experts_backward', out_shape=(jax.ShapeDtype...  71.7 us
    pallas_call x1, Pallas kernels, body(): pl.pallas_call(place, name='place_results', out_shape=(jax.ShapeDtypeStru...  1.68 us

profile of v2, /device:TPU:1, one launch (start us, length us, event | category | flops | bytes accessed | tf_op | source)
XLA Modules:
  0.0 74.0 jit_solution(306806091913460706)
XLA Ops:
  0.6 71.7 %experts_backward.1 = (f32[2,56,128]{2,1,0:T(8,128)}, f32[2,128]{1,0:T(2,128)}, f32[8,128]{1,0:T(8,128)}, bf16[384,128]{1,0:T(8,128)(2,1)}, bf16[384,128]{1,0:T(8,128)(2,1)}) custom-call(bf16[384,7168]{1,0:T(8,128)(2,1)} %u_hbm.1, bf16[14336,128]{1,0:T(8,128)(2,1)} %bitcast.5, bf16[384,128]{1,0:T(8,128)(2,1)} %gate_hbm.1, bf16[384,128]{1,0:T(8,128)(2,1)} %up_hbm.1, ...), custom_call_target="tpu_custom_call" | custom-call | tf_op jit(solution)/shard_map/experts_backward/pallas_call | solution.py:347
  72.3 1.7 %place_results.1 = (f32[56,2,128]{2,1,0:T(2,128)}, f32[1,2]{1,0:T(1,128)}, f32[3,128]{1,0:T(4,128)}, bf16[384,128]{1,0:T(8,128)(2,1)}, bf16[384,128]{1,0:T(8,128)(2,1)}) custom-call(f32[2,56,128]{2,1,0:T(8,128)} %get-tuple-element.15.down_ref, f32[2,128]{1,0:T(2,128)} %get-tuple-element.16.rms_ref, f32[8,128]{1,0:T(8,128)} %get-tuple-element.17.pgrad_ref, ...), custom_call_target="tpu_custom_call" | custom-call | tf_op jit(solution)/shard_map/place_results/pallas_call | solution.py:394

commit v3 on v2

--- a/solution.py
+++ b/solution.py
@@ -26,6 +26,14 @@
     far = 4 - (j + 1) // 2
     odd = j % 2
     return (odd * far + (1 - odd) * (8 - far)) % 8
+
+
+def ring_from(at):
+    return lambda t: (at + ring_offset(t)) % SIDE
+
+
+def starts_plus(j):
+    return ((j + 3) % SIDE) // 4
 
 
 def across(row):
@@ -107,14 +115,17 @@
         total = total + jnp.dot(hot, both, preferred_element_type=F32)
     wp[...] = total.astype(BF16)
 
-    @pl.loop(0, SIDE)
-    def _(i):
+    def gradient(i):
         block_copy(i).wait()
         yi = (y + ring_offset(i)) % SIDE
         value = lax.dot_general(
             ub[i], wp[...], (((0,), (0,)), ((), ())), preferred_element_type=F32
         )
         g[pl.ds(yi * SIDE, SIDE)] = value.reshape(SIDE, 2, PIECE, 2 * F)
+
+    @pl.loop(0, 3)
+    def _(i):
+        gradient(i)
 
     pl.semaphore_wait(barrier, 4 * (SIDE - 1) + 1)
 
@@ -132,15 +143,17 @@
 
     other_p, other_q = q, p
 
-    @pl.loop(0, SIDE)
-    def _(j):
+    def pair_lead(j):
         pair_copy(0, j, j).start()
-
-    @pl.loop(1, SIDE)
-    def _(r):
+        pair_copy(1 + starts_plus(j), j, SIDE + j).start()
+
+    def pair_rest(j):
+        pair_copy(2 - starts_plus(j), j, 2 * SIDE).start()
+
+    def pair_group(r):
         @pl.loop(0, SIDE)
         def _(j):
-            pair_copy(r, j, SIDE - 1 + r).start()
+            pair_copy(r, j, 2 * SIDE - 2 + r).start()
 
     def pair_wait(sem, pieces):
         part = r0.at[pl.ds(0, pieces)]
@@ -149,10 +162,9 @@
     def slot(d, k, j):
         return 6 * SIDE + j if k == 4 else (d * 3 + k - 1) * SIDE + j
 
-    def first_copy(d, k, j, idx):
+    def ring_copy(d, s, idx):
         step = 1 if d == 0 else SIDE - 1
         to = (a * ((p + step) % SIDE) + b * q) * 2 + c
-        s = slot(d, k, j)
         return pltpu.make_async_remote_copy(
             src_ref=r0.at[idx],
             dst_ref=rc1.at[s],
@@ -162,16 +174,27 @@
             device_id_type=MESH,
         )
 
-    def first_send(d, k, j, more):
+    def first_copy(d, k, j, idx):
+        return ring_copy(d, slot(d, k, j), idx)
+
+    def lead_send(j):
+        m = starts_plus(j)
+        near = b * ((q + ring_offset(j)) % SIDE)
+        pair_wait(j, 1)
+        pair_wait(SIDE + j, 1)
+        for d, far, s in (
+            (0, p + 3 + m, m * slot(0, 4, j) + (1 - m) * slot(0, 3, j)),
+            (1, p + 4 + m, (1 - m) * slot(1, 4, j) + m * slot(1, 3, j)),
+        ):
+            idx = a * (far % SIDE) + near
+            r0[idx] = r0[idx] + g[idx, c]
+            ring_copy(d, s, idx).start()
+
+    def first_send(d, k, j):
         step = 1 if d == 0 else SIDE - 1
         idx = a * ((p + step * k) % SIDE) + b * ((q + ring_offset(j)) % SIDE)
-        if k == 4:
-            pair_wait(j, 1)
-        value = r0[idx] + g[idx, c]
-        if more:
-            first_copy(d, k + 1, j, idx).wait_recv()
-            value = value + rc1[slot(d, k + 1, j)]
-        r0[idx] = value
+        first_copy(d, k + 1, j, idx).wait_recv()
+        r0[idx] = r0[idx] + g[idx, c] + rc1[slot(d, k + 1, j)]
         first_copy(d, k, j, idx).start()
 
     def project(i):
@@ -182,47 +205,48 @@
         )
         pacc[...] += jnp.dot(ub[i], weight, preferred_element_type=F32)
 
-    @pl.loop(0, 4)
+    pair_lead(0)
+    pair_lead(1)
+
+    @pl.loop(3, SIDE)
+    def _(i):
+        gradient(i)
+        pair_lead(i - 1)
+        pair_rest(i - 3)
+
+        @pl.when(i >= 4)
+        def _():
+            lead_send(i - 4)
+
+    pair_lead(7)
+    lead_send(4)
+
+    @pl.loop(5, SIDE)
     def _(j):
-        first_send(0, 4, j + 4, False)
-        first_send(1, 4, j, False)
-
-    pair_wait(SIDE, SIDE)
-    pair_wait(SIDE + 1, SIDE)
-
-    @pl.loop(0, 4)
-    def _(j):
-        first_send(0, 3, j, False)
-        first_send(1, 3, j + 4, False)
+        pair_rest(j)
+
+    pair_group(3)
+    lead_send(5)
+    pair_group(4)
+    lead_send(6)
+    lead_send(7)
+
+    @pl.loop(5, SIDE)
+    def _(r):
+        pair_group(r)
 
     w_copy.wait()
     pacc[...] = jnp.zeros_like(pacc)
 
-    @pl.loop(0, 4)
-    def _(j):
-        first_send(0, 3, j + 4, True)
-        first_send(1, 3, j, True)
-        project(j)
-
-    pair_wait(SIDE + 2, SIDE)
-    pair_wait(SIDE + 3, SIDE)
-
-    @pl.loop(0, 4)
-    def _(j):
-        for h in range(2):
-            first_send(0, 2, 2 * j + h, True)
-            first_send(1, 2, (2 * j + h + 4) % SIDE, True)
-        project(j + 4)
-
-    def exchange(buf, mine, count, send, recv, where):
-        @pl.loop(1, count)
-        def _(o):
+    def exchange(buf, mine, count, send, recv, order, where):
+        @pl.loop(0, count - 1)
+        def _(t):
             pltpu.make_async_remote_copy(
                 src_ref=buf.at[mine],
                 dst_ref=buf.at[mine],
                 send_sem=send,
                 recv_sem=recv,
-                device_id=where((mine + o) % count),
+                device_id=where(order(t)),
                 device_id_type=MESH,
             ).start()
 
@@ -230,41 +254,32 @@
         part = buf.at[pl.ds(0, count - 1)]
         pltpu.make_async_copy(part, part, sem).wait()
 
-    high = pacc[...].astype(BF16)
-    rest = pacc[...] - high.astype(F32)
-    middle = rest.astype(BF16)
-    low = (rest - middle.astype(F32)).astype(BF16)
-    pslot[x] = jnp.zeros((8, F), F32)
-    for k in range(NBLK):
-        rows = pl.ds(k * BLOCK, BLOCK)
-        hot = oh[k]
-        moved = sum(
-            lax.dot_general(hot, term, (((0,), (0,)), ((), ())), preferred_element_type=F32)
-            for term in (low, middle, high)
-        )
-        expert = jnp.full((F, F), expert_ref[k], jnp.int32)
-        projected = jnp.where(expert == 0, moved[:, :F], moved[:, F:])
-        gate = gate_ref[rows, :].astype(F32)
-        up = up_ref[rows, :].astype(F32)
-        sig = jax.nn.sigmoid(gate)
-        active = gate * sig
-        scaled = across(prob_ref[pl.ds(k, 1), :]) * projected
-        ugrad_ref[rows, :] = (scaled * active).astype(BF16)
-        ggrad_ref[rows, :] = (scaled * up * sig * (1.0 + gate * (1.0 - sig))).astype(BF16)
-        part = jnp.transpose(active * up * projected)
-        pslot[x, pl.ds(k, 1), :] = jnp.sum(part, axis=0, keepdims=True)
-
-    exchange(pslot, x, SIDE, p_send, p_recv, lambda to: (to, wide))
-
-    pair_wait(SIDE + 4, SIDE)
-    pair_wait(SIDE + 5, SIDE)
-
-    @pl.loop(0, SIDE)
-    def _(j):
-        first_send(0, 1, j, True)
-        first_send(1, 1, j, True)
-
-    pair_wait(SIDE + 6, SIDE)
+    def rows_back():
+        high = pacc[...].astype(BF16)
+        rest = pacc[...] - high.astype(F32)
+        middle = rest.astype(BF16)
+        low = (rest - middle.astype(F32)).astype(BF16)
+        pslot[x] = jnp.zeros((8, F), F32)
+        for k in range(NBLK):
+            rows = pl.ds(k * BLOCK, BLOCK)
+            hot = oh[k]
+            moved = sum(
+                lax.dot_general(hot, term, (((0,), (0,)), ((), ())), preferred_element_type=F32)
+                for term in (low, middle, high)
+            )
+            expert = jnp.full((F, F), expert_ref[k], jnp.int32)
+            projected = jnp.where(expert == 0, moved[:, :F], moved[:, F:])
+            gate = gate_ref[rows, :].astype(F32)
+            up = up_ref[rows, :].astype(F32)
+            sig = jax.nn.sigmoid(gate)
+            active = gate * sig
+            scaled = across(prob_ref[pl.ds(k, 1), :]) * projected
+            ugrad_ref[rows, :] = (scaled * active).astype(BF16)
+            ggrad_ref[rows, :] = (scaled * up * sig * (1.0 + gate * (1.0 - sig))).astype(BF16)
+            part = jnp.transpose(active * up * projected)
+            pslot[x, pl.ds(k, 1), :] = jnp.sum(part, axis=0, keepdims=True)
+
+        exchange(pslot, x, SIDE, p_send, p_recv, ring_from(x), lambda to: (to, wide))
 
     def second_slot(d, k):
         return d * 4 + k - 1
@@ -288,16 +303,49 @@
         first_copy(1, 1, j, idx).wait_recv()
         return idx, r0[idx] + g[idx, c] + rc1[slot(0, 1, j)] + rc1[slot(1, 1, j)]
 
-    for j, d, k, more in (
-        (0, 0, 4, False), (2, 1, 3, False), (1, 0, 3, True), (4, 1, 2, True),
-        (3, 0, 2, True), (6, 1, 1, True), (5, 0, 1, True),
-    ):
+    def second_send(j, d, k):
         idx, value = own(j)
-        if more:
+        if (d, k) not in ((0, 4), (1, 3)):
             second_copy(d, k + 1, idx).wait_recv()
             value = value + rc2[second_slot(d, k + 1)]
         r0[idx] = value
         second_copy(d, k, idx).start()
+
+    plus = (
+        (2, 0), (3, 2), (3, 1), (3, 4), (1, 0), (2, 2), (2, 1), (2, 4), (3, 3), (1, 2),
+        (1, 1), (1, 4), (2, 3), (2, 6), (2, 5), (2, 7), (1, 3), (1, 6), (1, 5), (1, 7),
+    )
+    minus = (
+        (3, 0), (2, 2), (2, 1), (2, 4), (2, 0), (1, 2), (1, 1), (1, 4), (1, 0), (2, 3),
+        (3, 6), (3, 5), (3, 7), (1, 3), (2, 6), (2, 5), (2, 7), (1, 6), (1, 5), (1, 7),
+    )
+    for n in range(len(plus)):
+        if n == 0:
+            for r in (2, 3, 4):
+                pair_wait(2 * SIDE - 2 + r, SIDE)
+        if n == 4:
+            for r in (5, 6):
+                pair_wait(2 * SIDE - 2 + r, SIDE)
+        first_send(0, *plus[n])
+        first_send(1, *minus[n])
+        if n in (0, 2, 4, 6):
+            @pl.loop(n, n + 2)
+            def _(i):
+                project(i)
+        if n == 8:
+            rows_back()
+        if n == 14:
+            pair_wait(3 * SIDE - 3, SIDE)
+            second_send(0, 0, 4)
+        if n == 15:
+            second_send(2, 1, 3)
+        if n == 16:
+            second_send(1, 0, 3)
+        if n == 18:
+            second_send(4, 1, 2)
+    second_send(3, 0, 2)
+    second_send(6, 1, 1)
+    second_send(5, 0, 1)
     idx, value = own(7)
     for d in range(2):
         second_copy(d, 1, idx).wait_recv()
@@ -308,13 +356,23 @@
     square = jnp.concatenate([column[:, :F], column[:, F:]], axis=0)
 
     stages = (
-        (qxc, x * 2 + c, 2 * SIDE, xc_send, xc_recv, lambda to: (to // 2, chip * 2 + to % 2)),
-        (qy, y, SIDE, y_send, y_recv, lambda to: (x, (to * SIDE + z) * 2 + c)),
-        (qz, z, SIDE, z_send, z_recv, lambda to: (x, (y * SIDE + to) * 2 + c)),
+        (
+            qxc, x * 2 + c, 2 * SIDE, xc_send, xc_recv,
+            lambda t: ((x + ring_offset(t // 2)) % SIDE) * 2 + (c + 1 + t) % 2,
+            lambda to: (to // 2, chip * 2 + to % 2),
+        ),
+        (
+            qy, y, SIDE, y_send, y_recv, ring_from(y),
+            lambda to: (x, (to * SIDE + z) * 2 + c),
+        ),
+        (
+            qz, z, SIDE, z_send, z_recv, ring_from(z),
+            lambda to: (x, (y * SIDE + to) * 2 + c),
+        ),
     )
-    for buf, mine, count, send, recv, where in stages:
+    for buf, mine, count, send, recv, order, where in stages:
         buf[mine] = square
-        exchange(buf, mine, count, send, recv, where)
+        exchange(buf, mine, count, send, recv, order, where)
         exchanged(buf, count, recv)
         square = jnp.sum(buf[...], axis=0)
     mean = jnp.sum(square, axis=1, keepdims=True) / float(D * FFW)
@@ -324,7 +382,7 @@
     pgrad_ref[...] = jnp.sum(pslot[...], axis=0)
 
     exchanged(pslot, SIDE, p_send)
-    for buf, _, count, send, _, _ in stages:
+    for buf, _, count, send, _, _, _ in stages:
         exchanged(buf, count, send)
     pltpu.make_async_copy(r0, r0, pair_send).wait()
     pltpu.make_async_copy(r0.at[pl.ds(0, 63)], r0.at[pl.ds(0, 63)], ring_send).wait()
@@ -376,7 +434,7 @@
             pltpu.VMEM((2 * SIDE, 2, F), F32),
             pltpu.VMEM((SIDE, 2, F), F32),
             pltpu.VMEM((SIDE, 2, F), F32),
-            dma((5,)), dma((SIDE,)), dma, dma, dma((2 * SIDE - 1,)), dma, dma((56,)), dma((8,)),
+            dma((5,)), dma((SIDE,)), dma, dma, dma((3 * SIDE - 2,)), dma, dma((56,)), dma((8,)),
             dma, dma, dma, dma, dma, dma, dma, dma,
         ],
         compiler_params=pltpu.CompilerParams(

time: 74.2 us -> 71.3 us (0.961)
  Pallas kernels: 73.4 us -> 70.2 us
    pallas_call x1, Pallas kernels: 71.7 us -> 68.6 us  [body(): pl.pallas_call(kernel, name='experts_backward', out_shape=(jax.ShapeDtype...]
where the time goes in v3:
time: 71.3 us; the launch traced here: 70.9 us
  Pallas kernels  70.2 us (98%)
    pallas_call x1, Pallas kernels, body(): pl.pallas_call(kernel, name='experts_backward', out_shape=(jax.ShapeDtype...  68.6 us
    pallas_call x1, Pallas kernels, body(): pl.pallas_call(place, name='place_results', out_shape=(jax.ShapeDtypeStru...  1.68 us

profile of v3, /device:TPU:1, one launch (start us, length us, event | category | flops | bytes accessed | tf_op | source)
XLA Modules:
  0.0 70.9 jit_solution(12531359696757279438)
XLA Ops:
  0.6 68.6 %experts_backward.1 = (f32[2,56,128]{2,1,0:T(8,128)}, f32[2,128]{1,0:T(2,128)}, f32[8,128]{1,0:T(8,128)}, bf16[384,128]{1,0:T(8,128)(2,1)}, bf16[384,128]{1,0:T(8,128)(2,1)}) custom-call(bf16[384,7168]{1,0:T(8,128)(2,1)} %u_hbm.1, bf16[14336,128]{1,0:T(8,128)(2,1)} %bitcast.5, bf16[384,128]{1,0:T(8,128)(2,1)} %gate_hbm.1, bf16[384,128]{1,0:T(8,128)(2,1)} %up_hbm.1, ...), custom_call_target="tpu_custom_call" | custom-call | tf_op jit(solution)/shard_map/experts_backward/pallas_call | solution.py:405
  69.2 1.7 %place_results.1 = (f32[56,2,128]{2,1,0:T(2,128)}, f32[1,2]{1,0:T(1,128)}, f32[3,128]{1,0:T(4,128)}, bf16[384,128]{1,0:T(8,128)(2,1)}, bf16[384,128]{1,0:T(8,128)(2,1)}) custom-call(f32[2,56,128]{2,1,0:T(8,128)} %get-tuple-element.15.down_ref, f32[2,128]{1,0:T(2,128)} %get-tuple-element.16.rms_ref, f32[8,128]{1,0:T(8,128)} %get-tuple-element.17.pgrad_ref, ...), custom_call_target="tpu_custom_call" | custom-call | tf_op jit(solution)/shard_map/place_results/pallas_call | solution.py:452

commit v4 on v3

--- a/solution.py
+++ b/solution.py
@@ -79,7 +79,6 @@
         block_copy(i).start()
 
     w_copy = pltpu.make_async_copy(w_hbm, wv, wsem)
-    w_copy.start()
 
     barrier = pltpu.get_barrier_semaphore()
 
@@ -127,6 +126,7 @@
     def _(i):
         gradient(i)
 
+    w_copy.start()
     pl.semaphore_wait(barrier, 4 * (SIDE - 1) + 1)
 
     def pair_copy(r, j, sem):

time: 71.3 us -> 71.3 us (level)
  no operation moved by 1% of the time
where the time goes in v4:
time: 71.3 us; the launch traced here: 70.9 us
  Pallas kernels  70.2 us (98%)
    pallas_call x1, Pallas kernels, body(): pl.pallas_call(kernel, name='experts_backward', out_shape=(jax.ShapeDtype...  68.6 us
    pallas_call x1, Pallas kernels, body(): pl.pallas_call(place, name='place_results', out_shape=(jax.ShapeDtypeStru...  1.68 us

profile of v4, /device:TPU:1, one launch (start us, length us, event | category | flops | bytes accessed | tf_op | source)
XLA Modules:
  0.0 70.9 jit_solution(10469739598047566539)
XLA Ops:
  0.6 68.6 %experts_backward.1 = (f32[2,56,128]{2,1,0:T(8,128)}, f32[2,128]{1,0:T(2,128)}, f32[8,128]{1,0:T(8,128)}, bf16[384,128]{1,0:T(8,128)(2,1)}, bf16[384,128]{1,0:T(8,128)(2,1)}) custom-call(bf16[384,7168]{1,0:T(8,128)(2,1)} %u_hbm.1, bf16[14336,128]{1,0:T(8,128)(2,1)} %bitcast.5, bf16[384,128]{1,0:T(8,128)(2,1)} %gate_hbm.1, bf16[384,128]{1,0:T(8,128)(2,1)} %up_hbm.1, ...), custom_call_target="tpu_custom_call" | custom-call | tf_op jit(solution)/shard_map/experts_backward/pallas_call | solution.py:405
  69.2 1.7 %place_results.1 = (f32[56,2,128]{2,1,0:T(2,128)}, f32[1,2]{1,0:T(1,128)}, f32[3,128]{1,0:T(4,128)}, bf16[384,128]{1,0:T(8,128)(2,1)}, bf16[384,128]{1,0:T(8,128)(2,1)}) custom-call(f32[2,56,128]{2,1,0:T(8,128)} %get-tuple-element.15.down_ref, f32[2,128]{1,0:T(2,128)} %get-tuple-element.16.rms_ref, f32[8,128]{1,0:T(8,128)} %get-tuple-element.17.pgrad_ref, ...), custom_call_target="tpu_custom_call" | custom-call | tf_op jit(solution)/shard_map/place_results/pallas_call | solution.py:452
